TPU v7x, 32 devices: a whole 2x2x4 slice. The times are simulated.
32 devices in a mesh: fiber: 16 (over z, y, x), wave: 2 (over core).
Axes of the slice: x: 2, y: 2, z: 4, core: 2. Of those that a mesh axis runs over, the one named last changes fastest.
Arguments:
- spectra: float32 [4, 640, 8192], P(None, 'fiber', 'wave'), may hold values from 0 to 10
- inverse_var: float32 [4, 640, 8192], P(None, 'fiber', 'wave'), may hold values from 0.1 to 10
- mask_bits: int32 [4, 640, 8192], P(None, 'fiber', 'wave'), may hold values from 0 to 512, as said below
- sky_flags: int32 [4, 640], P(None, 'fiber'), may hold values 0 or 1
- fiber_ids: int32 [640], P('fiber'), may hold values from 0 to 639, each once
- positions: float32 [2, 640], replicated, may hold values from -1 to 1
- throughput: float32 [4, 640], P(None, 'fiber'), may hold values from 0.5 to 1.5
Outputs:
- residual: float32 [4, 640, 8192], P(None, 'fiber', 'wave')
- chi_square: float32 [4, 640], P(None, 'fiber')
- sky_coeffs: float32 [16, 8192], P(None, 'wave')
Inputs may be any that keep to these rules, and one draw needn't show every extreme that they name: `mask_bits`: each entry is zero or one single bit of 0 to 9. `fiber_ids`: each fiber id appears in exactly one slot.
All inputs are finite; a program needn't handle non-finite values. No bound on the sum of `sky_flags` on one device may be relied on, other than what follows from the above.
Results may differ from a plain program's by a relative error of at most 0.0003.
Values sent between devices are 32-bit elements; how exact they have to be, the bound alone decides.
A program may use at most 64 MiB of HBM per device.

v0:
```python
import jax
import jax.numpy as jnp
from jax import lax
from jax.sharding import PartitionSpec as P

PARAMS = 16


bad_bits = 31
prior_weight = 1.0
highest = lax.Precision.HIGHEST
moment_degrees = 7
basis_degrees = 4


def legendre(coord):
    return [
        jnp.ones_like(coord),
        coord,
        1.5 * coord * coord - 0.5,
        (2.5 * coord * coord - 1.5) * coord,
    ]


def legendre_series(coord, degree_total):
    series = [jnp.ones_like(coord), coord]
    for order in range(1, degree_total - 1):
        series.append(
            ((2 * order + 1) * coord * series[order] - order * series[order - 1]) / (order + 1)
        )
    return series


def build_design(positions, fiber_ids, throughput):
    coord_x = positions[0][fiber_ids]
    coord_y = positions[1][fiber_ids]
    poly_x = legendre(coord_x)
    poly_y = legendre(coord_y)
    basis = jnp.stack([along_x * along_y for along_x in poly_x for along_y in poly_y], axis=-1)
    return throughput[:, :, None] * basis[None]


def moment_features(positions, fiber_ids, throughput):
    coord_x = positions[0][fiber_ids]
    coord_y = positions[1][fiber_ids]
    series_x = legendre_series(coord_x, moment_degrees)
    series_y = legendre_series(coord_y, moment_degrees)
    basis = jnp.stack([along_x * along_y for along_x in series_x for along_y in series_y], axis=-1)
    return (throughput * throughput)[:, :, None] * basis[None]


def monomial_table(degree_total):
    coeffs = [[0.0] * degree_total for order in range(degree_total)]
    coeffs[0][0] = 1.0
    coeffs[1][1] = 1.0
    for order in range(1, degree_total - 1):
        for power in range(degree_total):
            raised = coeffs[order][power - 1] if power >= 1 else 0.0
            coeffs[order + 1][power] = (
                (2 * order + 1) * raised - order * coeffs[order - 1][power]
            ) / (order + 1)
    return coeffs


def product_series(higher, first, second):
    product = [0.0] * moment_degrees
    for left_power in range(moment_degrees):
        for right_power in range(moment_degrees - left_power):
            product[left_power + right_power] += (
                higher[first][left_power] * higher[second][right_power]
            )
    series = [0.0] * moment_degrees
    for order in reversed(range(moment_degrees)):
        weight_now = product[order] / higher[order][order]
        series[order] = weight_now
        for power in range(moment_degrees):
            product[power] -= weight_now * higher[order][power]
    return series


def rebuild_table():
    higher = monomial_table(moment_degrees)
    pair_coeffs = [
        [product_series(higher, first, second) for second in range(basis_degrees)]
        for first in range(basis_degrees)
    ]
    table_rows = []
    for index_i in range(basis_degrees):
        for index_j in range(basis_degrees):
            for index_k in range(basis_degrees):
                for index_l in range(basis_degrees):
                    table_rows.append(
                        [
                            pair_coeffs[index_i][index_k][order_a]
                            * pair_coeffs[index_j][index_l][order_b]
                            for order_a in range(moment_degrees)
                            for order_b in range(moment_degrees)
                        ]
                    )
    return jnp.asarray(table_rows, jnp.float32)


def solve_normal(matrix, right_side):
    param_count = right_side.shape[0]
    factor = {}
    for column in range(param_count):
        pivot_sum = matrix[column * param_count + column] + prior_weight
        for inner_k in range(column):
            pivot_sum = pivot_sum - factor[column, inner_k] * factor[column, inner_k]
        root_value = jnp.sqrt(pivot_sum)
        factor[column, column] = root_value
        for target in range(column + 1, param_count):
            running = matrix[target * param_count + column]
            for inner_k in range(column):
                running = running - factor[target, inner_k] * factor[column, inner_k]
            factor[target, column] = running / root_value
    interim = []
    for target in range(param_count):
        running = right_side[target]
        for inner_k in range(target):
            running = running - factor[target, inner_k] * interim[inner_k]
        interim.append(running / factor[target, target])
    solved = [None] * param_count
    for target in reversed(range(param_count)):
        running = interim[target]
        for inner_k in range(target + 1, param_count):
            running = running - factor[inner_k, target] * solved[inner_k]
        solved[target] = running / factor[target, target]
    return jnp.stack(solved)


def expand_normal(normal):
    return jnp.dot(rebuild_table(), normal, precision=highest)


def body(spectra, inverse_var, mask_bits, sky_flags, fiber_ids, positions, throughput):
    exposures, fiber_count, wave_count = spectra.shape
    row_count = exposures * fiber_count
    design = build_design(positions, fiber_ids, throughput).reshape(row_count, PARAMS)
    flux_rows = spectra.reshape(row_count, wave_count)
    usable = (mask_bits.reshape(row_count, wave_count) & bad_bits == 0).astype(jnp.float32)
    noise_weight = inverse_var.reshape(row_count, wave_count) * usable
    fit_weights = noise_weight * sky_flags.reshape(row_count).astype(jnp.float32)[:, None]
    products = moment_features(positions, fiber_ids, throughput).reshape(
        row_count, moment_degrees * moment_degrees
    )
    normal = jnp.dot(products.T, fit_weights, precision=highest)
    right_side = jnp.dot(design.T, fit_weights * flux_rows, precision=highest)
    normal, right_side = lax.psum((normal, right_side), "fiber")
    normal = expand_normal(normal)
    sky_coeffs = solve_normal(normal, right_side)
    residual = flux_rows - jnp.dot(design, sky_coeffs, precision=highest)
    chi_local = jnp.sum(noise_weight * residual * residual, axis=1)
    chi_total = lax.psum(chi_local, "wave")
    chi_square = (chi_total / (wave_count * lax.axis_size("wave"))).reshape(exposures, fiber_count)
    return (residual.reshape(exposures, fiber_count, wave_count), chi_square, sky_coeffs)


def solution(mesh):
    placed = (
        P(None, "fiber", "wave"),
        P(None, "fiber", "wave"),
        P(None, "fiber", "wave"),
        P(None, "fiber"),
        P("fiber"),
        P(),
        P(None, "fiber"),
    )
    return jax.shard_map(
        body,
        mesh=mesh,
        in_specs=placed,
        out_specs=(P(None, "fiber", "wave"), P(None, "fiber"), P(None, "wave")),
        check_vma=False,
    )
```

profile of v0, /device:TPU:0, one launch (start us, length us, event | category | flops | bytes accessed | tf_op | source)
XLA Modules:
  0.0 187.3 jit_solution(226238321649454754)
XLA Ops:
  7.2 0.8 slice_reduce_fusion
  8.0 0.7 compare_select_fusion
  8.7 0.7 gather_fusion
  9.4 0.7 gather_fusion.1
  10.1 0.8 mul.18449
  11.0 0.7 broadcast_multiply_fusion
  11.7 0.7 convert_element_type.8
  12.6 3.0 %fusion.2 = f32[4,40,4096]{2,1,0:T(8,128)S(1)} fusion(f32[4,40,4096]{2,1,0:T(8,128)} %param.9, s32[4,40,4096]{2,1,0:T(8,128)} %param.10), kind=kLoop, calls=%fused_computation.9 | loop fusion | flops 1966080 | bytes 7864320 | tf_op jit(solution)/shard_map/mul | solution.py:142
  15.9 2.6 %convolution_bitcast_fusion.1 = f32[16,4096]{1,0:T(8,128)} fusion(f32[4,40,4096]{2,1,0:T(8,128)S(1)} %copy-done, f32[4,40,4096]{2,1,0:T(8,128)S(1)} %fusion.2, f32[4,40]{1,0:T(4,128)S(1)} %convert_element_type.8, f32[4,40,16]{1,0,2:T(4,128)S(1)} %broadcast_multiply_fusion), kind=kOutput, calls=%fused_computation.4 | convolution fusion | flops 127139840 | bytes 5515904 | tf_op jit(solution)/shard_map/dot_general | solution.py:148
  18.5 2.7 %convolution_bitcast_fusion = f32[49,4096]{1,0:T(8,128)} fusion(f32[4,40,4096]{2,1,0:T(8,128)S(1)} %fusion.2, f32[4,40]{1,0:T(4,128)S(1)} %convert_element_type.8, f32[40,49]{1,0:T(8,128)S(1)} %copy.13, f32[4,40]{1,0:T(4,128)S(1)} %mul.18449), kind=kOutput, calls=%fused_computation.3 | convolution fusion | flops 386014880 | bytes 3433376 | tf_op jit(solution)/shard_map/dot_general | solution.py:147
  21.3 116.4 %all-reduce.3.cloned.1.call-done = (f32[49,4096]{1,0:T(8,128)}, f32[16,4096]{1,0:T(8,128)}) async-done(((f32[49,4096]{1,0:T(8,128)}, f32[16,4096]{1,0:T(8,128)}), (f32[49,4096]{1,0:T(8,128)}, f32[16,4096]{1,0:T(8,128)})) %all-reduce.3.cloned.1.call-update) | async-done | bytes 1064976 | tf_op jit(solution)/shard_map/psum | solution.py:149
  137.8 4.6 %fusion.83 = f32[256,4096]{1,0:T(8,128)S(1)} fusion(f32[256,49]{1,0:T(8,128)S(1)} %copy-done.3, f32[49,4096]{1,0:T(8,128)} %get-tuple-element.5), kind=kOutput, calls=%fused_computation.468 | convolution fusion | flops 616562688 | bytes 5047296 | tf_op jit(solution)/shard_map/dot_general | solution.py:133
  142.4 1.4 subtract_divide_fusion.104
  146.0 2.1 %subtract_divide_fusion.143 = (f32[4096]{0:T(1024)S(1)}, f32[4096]{0:T(1024)S(1)}, f32[4096]{0:T(1024)S(1)}, f32[4096]{0:T(1024)S(1)}, f32[4096]{0:T(1024)S(1)},...) fusion(f32[4096]{0:T(1024)S(1)} %bitcast.709, ...), kind=kLoop, calls=%fused_computation.193 | loop fusion | flops 7176192 | bytes 3653632 | tf_op jit(solution)/shard_map/div | solution.py:128
  148.2 1.4 subtract_divide_fusion.144
  149.6 1.4 subtract_divide_fusion.145
  151.1 1.9 %subtract_divide_fusion.133 = (f32[4096]{0:T(1024)S(1)}, f32[4096]{0:T(1024)S(1)}) fusion(f32[4096]{0:T(1024)S(1)} %get-tuple-element.222, f32[4096]{0:T(1024)S(1)} %get-tuple-element.180, f32[4096]{0:T(1024)S(1)} %subtract_divide_fusion.145, f32[4096]{0:T(1024)S(1)} %get-tuple-element.200, f32[4096]{0:T(1024)S(1)} %subtract_divide_fusion.144, ...), kind=kLoop, calls=%fused_computation.183 | loop fusion | flops 6492160 | bytes 2523136 | tf_op jit(solution)/shard_map/div | solution.py:128
  153.0 1.7 subtract_divide_fusion.131
  154.7 10.1 %subtract_divide_fusion.26 = (f32[1,4096]{1,0:T(1,128)S(1)}, f32[1,4096]{1,0:T(1,128)S(1)}, f32[1,4096]{1,0:T(1,128)S(1)}, f32[1,4096]{1,0:T(1,128)S(1)}, f32[1,...) fusion(f32[16,4096]{1,0:T(8,128)S(1)} %copy-done.1, ...), kind=kLoop, calls=%fused_computation.63 | loop fusion | flops 5423104 | bytes 3751936 | tf_op jit(solution)/shard_map/div | solution.py:122
  164.8 3.2 %subtract_divide_fusion.12 = (f32[1,4096]{1,0:T(1,128)S(1)}, f32[1,4096]{1,0:T(1,128)S(1)}, f32[1,4096]{1,0:T(1,128)S(1)}, f32[1,4096]{1,0:T(1,128)S(1)}, f32[1,...) fusion(f32[1,4096]{1,0:T(1,128)S(1)} %get-tuple-element.35, ...), kind=kLoop, calls=%fused_computation.48 | loop fusion | flops 1511424 | bytes 2457600 | tf_op jit(solution)/shard_map/div | solution.py:116
  168.0 3.2 %subtract_divide_fusion = (f32[1,4096]{1,0:T(1,128)S(1)}, f32[1,4096]{1,0:T(1,128)S(1)}, f32[1,4096]{1,0:T(1,128)S(1)}, f32[1,4096]{1,0:T(1,128)S(1)}, f32[1,409...) fusion(f32[1,4096]{1,0:T(1,128)S(1)} %get-tuple-element.125, ...), kind=kLoop, calls=%fused_computation.35 | loop fusion | flops 1499136 | bytes 2457600 | tf_op jit(solution)/shard_map/div | solution.py:128
  171.6 5.8 %fusion = (f32[160]{0:T(256)S(1)}, f32[160,4096]{1,0:T(8,128)}) fusion(f32[160,4096]{1,0:T(8,128)S(1)} %bitcast.379, f32[160,4096]{1,0:T(8,128)} %bitcast.380, f32[16,4096]{1,0:T(8,128)S(1)} %stack.23, f32[160,16]{0,1:T(8,128)S(1)} %mul.18441, f32[160]{0:T(256)S(1)} %mul.18419), kind=kOutput, calls=%fused_computation.6 | convolution fusion | flops 128452960 | bytes 8137984 | tf_op jit(solution)/shard_map/dot_general | solution.py:152
  177.4 2.4 %psum.23 = f32[160]{0:T(256)S(1)} all-reduce(f32[160]{0:T(256)S(1)} %get-tuple-element.443), channel_id=1, replica_groups=mesh['fiber'=16,'wave'=2] {'wave'}, use_global_device_ids=true, to_apply=%region_3.0 | all-reduce | flops 160 | bytes 1280 | tf_op jit(solution)/shard_map/psum | solution.py:154
  179.8 0.7 reshape.825
  (32 shorter events, 3.4 us)
Async XLA Ops:
  7.2 130.6 %all-reduce.3.cloned.1.call-start = ((), (), s32[]{:S(2)}) async-start(), calls=%async_computation | async-start | bytes 2359296 | tf_op jit(solution)/shard_map/psum | solution.py:149
  12.6 3.3 %copy-start = (f32[4,40,4096]{2,1,0:T(8,128)S(1)}, f32[4,40,4096]{2,1,0:T(8,128)}, u32[]{:S(2)}) copy-start(f32[4,40,4096]{2,1,0:T(8,128)} %param.8) | copy-start | bytes 7864324
  18.5 2.7 %copy-start.4 = (f32[4,40]{1,0:T(4,128)S(1)}, f32[4,40]{1,0:T(4,128)}, u32[]{:S(2)}) copy-start(f32[4,40]{1,0:T(4,128)} %param.14) | copy-start | bytes 1924
  18.5 119.3 %copy-start.3 = (f32[256,49]{1,0:T(8,128)S(1)}, f32[256,49]{1,0:T(8,128)}, u32[]{:S(2)}) copy-start(f32[256,49]{1,0:T(8,128)} %constant.70.clone) | copy-start | bytes 150532
  142.4 3.4 %copy-start.1 = (f32[16,4096]{1,0:T(8,128)S(1)}, f32[16,4096]{1,0:T(8,128)}, u32[]{:S(2)}) copy-start(f32[16,4096]{1,0:T(8,128)} %get-tuple-element.6) | copy-start | bytes 786436
  171.5 5.8 %copy-start.2 = (f32[16,4096]{1,0:T(8,128)}, f32[16,4096]{1,0:T(8,128)S(1)}, u32[]{:S(2)}) copy-start(f32[16,4096]{1,0:T(8,128)S(1)} %stack.23) | copy-start | bytes 786436
Sparse Core Ops, SparseCore 0:
  21.3 116.4 all-reduce.2
where the time goes:
time: 188 us; the launch traced here: 187 us
  waiting for transfers between devices  116 us (62%)
  other arithmetic  34.3 us (18%)
  matrix products  15.7 us (8%)
  between operations  14.2 us (8%)
  local copies, waits for them, and re-layouts  4.25 us (2%)
  blocking collectives  2.44 us (1%)
    psum x1, waiting for transfers between devices, body(): normal, right_side = lax.psum((normal, right_side), 'fiber')  116 us
    div x6, other arithmetic, solve_normal(): solved[target] = running / factor[target, target]  11.8 us
    div x1, other arithmetic, solve_normal(): interim.append(running / factor[target, target])  10.1 us
    dot_general x1, matrix products, body(): residual = flux_rows - jnp.dot(design, sky_coeffs, precision=highest)  5.83 us
    div x3, other arithmetic, solve_normal(): factor[target, column] = running / root_value  4.7 us
    dot_general x1, matrix products, expand_normal(): return jnp.dot(rebuild_table(), normal, precision=highest)  4.63 us
  transfers between devices with their start and end apart: 1, of which 1 were waited for; matrix products, arithmetic and copies ran while one was open for 0% of the time, Pallas kernels for 0%

commit v1 on v0

v1 whole, which is shorter than its diff:
```python
import functools

import jax
import jax.numpy as jnp
from jax import lax
from jax.experimental import pallas as pl
from jax.experimental.pallas import tpu as pltpu
from jax.sharding import PartitionSpec as P

PARAMS = 16

bad_bits = 31
prior_weight = 1.0
highest = lax.Precision.HIGHEST
moment_degrees = 7
basis_degrees = 4
padded_degrees = 8
moment_rows = moment_degrees * padded_degrees
all_rows = moment_rows + PARAMS
lanes = 128
low_size = 4
MESH = pl.DeviceIdType.MESH


def monomial_table(degree_total):
    coeffs = [[0.0] * degree_total for order in range(degree_total)]
    coeffs[0][0] = 1.0
    coeffs[1][1] = 1.0
    for order in range(1, degree_total - 1):
        for power in range(degree_total):
            raised = coeffs[order][power - 1] if power >= 1 else 0.0
            coeffs[order + 1][power] = (
                (2 * order + 1) * raised - order * coeffs[order - 1][power]
            ) / (order + 1)
    return coeffs


def product_series(higher, first, second):
    product = [0.0] * moment_degrees
    for left_power in range(moment_degrees):
        for right_power in range(moment_degrees - left_power):
            product[left_power + right_power] += (
                higher[first][left_power] * higher[second][right_power]
            )
    series = [0.0] * moment_degrees
    for order in reversed(range(moment_degrees)):
        weight_now = product[order] / higher[order][order]
        series[order] = weight_now
        for power in range(moment_degrees):
            product[power] -= weight_now * higher[order][power]
    return series


def rebuild_table(row_degrees):
    higher = monomial_table(moment_degrees)
    pair = [
        [product_series(higher, first, second) for second in range(basis_degrees)]
        for first in range(basis_degrees)
    ]
    degrees = range(basis_degrees)
    return jnp.asarray(
        [
            [
                pair[i][k][a] * pair[j][l][b] if b < moment_degrees else 0.0
                for a in range(moment_degrees)
                for b in range(row_degrees)
            ]
            for i in degrees
            for j in degrees
            for k in degrees
            for l in degrees
        ],
        jnp.float32,
    )


def legendre(coord):
    return [
        jnp.ones_like(coord),
        coord,
        1.5 * coord * coord - 0.5,
        (2.5 * coord * coord - 1.5) * coord,
    ]


def legendre_series(coord, degree_total):
    series = [jnp.ones_like(coord), coord]
    for order in range(1, degree_total - 1):
        series.append(
            ((2 * order + 1) * coord * series[order] - order * series[order - 1]) / (order + 1)
        )
    return series


def exact_dot(left, right):
    return jnp.dot(left, right, precision=highest, preferred_element_type=jnp.float32)


def transposed_dot(left, right):
    return lax.dot_general(
        left, right, (((1,), (1,)), ((), ())), precision=highest, preferred_element_type=jnp.float32
    )


def split_bf16(value):
    high = value.astype(jnp.bfloat16)
    low = (value - high.astype(jnp.float32)).astype(jnp.bfloat16)
    return high, low


def iota(shape, axis):
    return lax.broadcasted_iota(jnp.int32, shape, axis)


def build_features(ids_ref, positions_ref, throughput_ref, flags_ref):
    exposures, fibers = throughput_ref.shape
    rows = exposures * fibers
    total = positions_ref.shape[1]
    pick = (iota((total, fibers), 0) == ids_ref[...]).astype(jnp.float32)
    coords = exact_dot(positions_ref[...], pick)
    column = iota((fibers, rows), 1)
    spread = functools.reduce(
        jnp.logical_or,
        [iota((fibers, rows), 0) + e * fibers == column for e in range(exposures)],
    ).astype(jnp.float32)
    at = iota((exposures, rows), 1) - iota((exposures, rows), 0) * fibers
    own = (at >= 0) & (at < fibers)

    def widen(value):
        return jnp.sum(jnp.where(own, exact_dot(value, spread), 0.0), axis=0, keepdims=True)

    coords = exact_dot(coords, spread)
    coord_x, coord_y = coords[0:1], coords[1:2]
    through = widen(throughput_ref[...])
    flags = widen(flags_ref[...].astype(jnp.float32))
    series_x = legendre_series(coord_x, moment_degrees)
    series_y = legendre_series(coord_y, moment_degrees)
    sub = iota((padded_degrees, rows), 0)
    stack_y = jnp.zeros((padded_degrees, rows), jnp.float32)
    for order in range(moment_degrees):
        stack_y = jnp.where(sub == order, series_y[order], stack_y)
    scale = through * through * flags
    moments = jnp.concatenate([stack_y * (one * scale) for one in series_x], axis=0)
    poly_x, poly_y = legendre(coord_x), legendre(coord_y)
    sub = iota((PARAMS, rows), 0)
    design = jnp.zeros((PARAMS, rows), jnp.float32)
    for k in range(PARAMS):
        value = poly_x[k // basis_degrees] * poly_y[k % basis_degrees]
        design = jnp.where(sub == k, value * through, design)
    return moments, design * flags, design


def solve_block(table, summed):
    width = summed.shape[1]
    normal = exact_dot(table, summed[:moment_rows])
    right = summed[moment_rows:]
    sub = iota((PARAMS, width), 0)
    cols = [
        normal[k * PARAMS:(k + 1) * PARAMS] + jnp.where(sub == k, prior_weight, 0.0)
        for k in range(PARAMS)
    ]
    factor, inverse, interim = [], [], []
    for k in range(PARAMS):
        pivot = cols[k][k:k + 1]
        root = lax.rsqrt(pivot)
        root = root * (1.5 - 0.5 * pivot * root * root)
        inverse.append(root)
        line = cols[k] * root
        factor.append(line)
        value = right[k:k + 1] * root
        interim.append(value)
        right = right - line * value
        for j in range(k + 1, PARAMS):
            cols[j] = cols[j] - line * line[j:j + 1]
    solved = jnp.zeros((PARAMS, width), jnp.float32)
    for k in reversed(range(PARAMS)):
        known = jnp.sum(jnp.where(sub > k, factor[k] * solved, 0.0), axis=0, keepdims=True)
        solved = jnp.where(sub == k, (interim[k] - known) * inverse[k], solved)
    return solved


def kernel(
    fiber_size, wave_size, slices,
    ids_ref, positions_ref, throughput_ref, flags_ref, table_ref,
    spectra_hbm, ivar_hbm, bits_hbm,
    residual_hbm, chi_ref, coeffs_ref,
    flux, noise, bits, resid, moments, gather1, partial, gather2, coeffs,
    chi_mine, chi_other,
    load_sem, store_sem, send_sem, recv_sem, chi_sem,
):
    exposures, fibers, waves = flux.shape
    rows = exposures * fibers
    high_size = fiber_size // low_size
    block = waves // (slices * fiber_size)
    chunk = high_size * block
    me = lax.axis_index("fiber")
    wave_me = lax.axis_index("wave")
    low, high = lax.rem(me, low_size), me // low_size
    low_peer = [high * low_size + lax.rem(low + d, low_size) for d in range(low_size)]
    high_peer = [lax.rem(high + d, high_size) * low_size + low for d in range(high_size)]

    barrier = pltpu.get_barrier_semaphore()
    for peer in low_peer[1:] + high_peer[1:]:
        pl.semaphore_signal(barrier, inc=1, device_id={"fiber": peer}, device_id_type=MESH)
    pl.semaphore_signal(barrier, inc=1, device_id={"wave": 1 - wave_me}, device_id_type=MESH)

    order = [(s, d) for s in range(slices) for d in list(range(1, low_size)) + [0]]

    def span(s, d):
        group = lax.rem(low + d, low_size)
        return group, pl.ds(pl.multiple_of(s * low_size * chunk + group * chunk, chunk), chunk)

    loads = []
    for at, (s, d) in enumerate(order):
        where = span(s, d)[1]
        copies = []
        for n, (source, target) in enumerate(
            ((spectra_hbm, flux), (ivar_hbm, noise), (bits_hbm, bits))
        ):
            copy = pltpu.make_async_copy(
                source.at[:, :, where], target.at[:, :, where], load_sem.at[at, n]
            )
            copy.start()
            copies.append(copy)
        loads.append(copies)

    feature, right_feature, design = build_features(
        ids_ref, positions_ref, throughput_ref, flags_ref
    )
    eye = (iota((rows, rows), 0) == iota((rows, rows), 1)).astype(jnp.float32)
    design_high, design_low = split_bf16(transposed_dot(eye, design))
    design_wide = jnp.concatenate([design_high, design_low, design_high], axis=1)

    pl.semaphore_wait(barrier, low_size - 1 + high_size - 1 + 1)

    def remote(stage, s, d, source, target, peer):
        return pltpu.make_async_remote_copy(
            src_ref=source, dst_ref=target,
            send_sem=send_sem.at[s, stage, d - 1], recv_sem=recv_sem.at[s, stage, d - 1],
            device_id={"fiber": peer}, device_id_type=MESH,
        )

    started = []
    first = {}
    for at, (s, d) in enumerate(order):
        group, where = span(s, d)
        for copy in loads[at]:
            copy.wait()
        good = (bits[:, :, where] & bad_bits) == 0
        weight = jnp.where(good, noise[:, :, where], 0.0)
        noise[:, :, where] = weight
        scaled = (weight * flux[:, :, where]).reshape(rows, chunk)
        normal = exact_dot(feature, weight.reshape(rows, chunk))
        right = exact_dot(right_feature, scaled)
        for b in range(high_size):
            lane = slice(b * block, (b + 1) * block)
            moments[s, group, b, :moment_rows] = normal[:, lane]
            moments[s, group, b, moment_rows:] = right[:, lane]
        if d:
            copy = remote(0, s, d, moments.at[s, group], gather1.at[s, d - 1], low_peer[d])
            copy.start()
            started.append(copy)
            first[s, d] = copy

    def reduce_low(s):
        for d in range(1, low_size):
            first[s, d].wait_recv()
        copies = []
        for d in list(range(1, high_size)) + [0]:
            to = lax.rem(high + d, high_size)
            total = moments[s, low, to]
            for e in range(low_size - 1):
                total = total + gather1[s, e, to]
            partial[s, to] = total
            if d:
                copy = remote(1, s, d, partial.at[s, to], gather2.at[s, d - 1], high_peer[d])
                copy.start()
                copies.append(copy)
        started.extend(copies)
        return copies

    def reduce_high(s, copies):
        for copy in copies:
            copy.wait_recv()
        total = partial[s, high]
        for e in range(high_size - 1):
            total = total + gather2[s, e]
        solved = solve_block(table_ref[...], total)
        mine = coeffs.at[s, low * high_size + high]
        mine[...] = solved
        copies = []
        for d in range(1, high_size):
            copy = remote(2, s, d, mine, mine, high_peer[d])
            copy.start()
            copies.append(copy)
        started.extend(copies)
        return copies

    def spread_low(s, copies):
        for copy in copies:
            copy.wait_recv()
        mine = coeffs.at[s, pl.ds(low * high_size, high_size)]
        copies = []
        for d in range(1, low_size):
            copy = remote(3, s, d, mine, mine, low_peer[d])
            copy.start()
            copies.append(copy)
        started.extend(copies)
        return copies

    stores = []
    chi_total = [jnp.zeros((rows, lanes), jnp.float32)]

    def finish(s, copies):
        for copy in copies:
            copy.wait_recv()
        for group in range(low_size):
            start = (s * low_size + group) * chunk
            where = pl.ds(start, chunk)
            values = jnp.concatenate(
                [coeffs[s, group * high_size + b] for b in range(high_size)], axis=1
            )
            coeffs_ref[:, where] = values
            value_high, value_low = split_bf16(values)
            model = jnp.dot(
                design_wide,
                jnp.concatenate([value_high, value_high, value_low], axis=0),
                preferred_element_type=jnp.float32,
            )
            left = flux[:, :, where].reshape(rows, chunk) - model
            resid[:, :, where] = left.reshape(exposures, fibers, chunk)
            term = noise[:, :, where].reshape(rows, chunk) * left * left
            for n in range(chunk // lanes):
                chi_total[0] = chi_total[0] + term[:, n * lanes:(n + 1) * lanes]
            copy = pltpu.make_async_copy(
                resid.at[:, :, where], residual_hbm.at[:, :, where],
                store_sem.at[s * low_size + group],
            )
            copy.start()
            stores.append(copy)

    stage = {}
    stage[0] = reduce_high(0, reduce_low(0))
    for s in range(1, slices):
        following = reduce_low(s)
        stage[s - 1] = spread_low(s - 1, stage[s - 1])
        stage[s] = reduce_high(s, following)
        finish(s - 1, stage[s - 1])
    finish(slices - 1, spread_low(slices - 1, stage[slices - 1]))

    chi_mine[...] = jnp.zeros_like(chi_mine)
    ones = jnp.ones((8, lanes), jnp.float32)
    for e in range(exposures):
        line = transposed_dot(ones, chi_total[0][e * fibers:(e + 1) * fibers])
        chi_mine[e:e + 1, :fibers] = line[0:1]
    copy = pltpu.make_async_remote_copy(
        src_ref=chi_mine, dst_ref=chi_other, send_sem=chi_sem.at[0], recv_sem=chi_sem.at[1],
        device_id={"wave": 1 - wave_me}, device_id_type=MESH,
    )
    copy.start()
    copy.wait()
    both = chi_mine[:exposures, :fibers] + chi_other[:exposures, :fibers]
    chi_ref[...] = both / (waves * wave_size)
    for copy in stores:
        copy.wait()
    for copy in started:
        copy.wait_send()


def fused_body(fiber_size, wave_size, slices, spectra, inverse_var, mask_bits, sky_flags,
               fiber_ids, positions, throughput):
    exposures, fibers, waves = spectra.shape
    high_size = fiber_size // low_size
    block = waves // (slices * fiber_size)
    table = rebuild_table(padded_degrees)
    vmem = pl.BlockSpec(memory_space=pltpu.VMEM)
    anywhere = pl.BlockSpec(memory_space=pl.ANY)
    cube = (exposures, fibers, waves)
    residual, chi, coeffs = pl.pallas_call(
        functools.partial(kernel, fiber_size, wave_size, slices),
        out_shape=(
            jax.ShapeDtypeStruct(cube, jnp.float32),
            jax.ShapeDtypeStruct((exposures, fibers), jnp.float32),
            jax.ShapeDtypeStruct((PARAMS, waves), jnp.float32),
        ),
        in_specs=[vmem] * 5 + [anywhere] * 3,
        out_specs=(anywhere, vmem, vmem),
        scratch_shapes=[
            pltpu.VMEM(cube, jnp.float32),
            pltpu.VMEM(cube, jnp.float32),
            pltpu.VMEM(cube, jnp.int32),
            pltpu.VMEM(cube, jnp.float32),
            pltpu.VMEM((slices, low_size, high_size, all_rows, block), jnp.float32),
            pltpu.VMEM((slices, low_size - 1, high_size, all_rows, block), jnp.float32),
            pltpu.VMEM((slices, high_size, all_rows, block), jnp.float32),
            pltpu.VMEM((slices, high_size - 1, all_rows, block), jnp.float32),
            pltpu.VMEM((slices, fiber_size, PARAMS, block), jnp.float32),
            pltpu.VMEM((8, lanes), jnp.float32),
            pltpu.VMEM((8, lanes), jnp.float32),
            pltpu.SemaphoreType.DMA((slices * low_size, 3)),
            pltpu.SemaphoreType.DMA((slices * low_size,)),
            pltpu.SemaphoreType.DMA((slices, 4, max(low_size, high_size) - 1)),
            pltpu.SemaphoreType.DMA((slices, 4, max(low_size, high_size) - 1)),
            pltpu.SemaphoreType.DMA((2,)),
        ],
        compiler_params=pltpu.CompilerParams(
            collective_id=0, has_side_effects=True, vmem_limit_bytes=40 * 1024 * 1024
        ),
    )(fiber_ids.reshape(1, fibers), positions, throughput, sky_flags, table,
      spectra, inverse_var, mask_bits)
    return residual, chi, coeffs


def solve_normal(matrix, right_side):
    param_count = right_side.shape[0]
    factor = {}
    for column in range(param_count):
        pivot_sum = matrix[column * param_count + column] + prior_weight
        for inner_k in range(column):
            pivot_sum = pivot_sum - factor[column, inner_k] * factor[column, inner_k]
        root_value = jnp.sqrt(pivot_sum)
        factor[column, column] = root_value
        for target in range(column + 1, param_count):
            running = matrix[target * param_count + column]
            for inner_k in range(column):
                running = running - factor[target, inner_k] * factor[column, inner_k]
            factor[target, column] = running / root_value
    interim = []
    for target in range(param_count):
        running = right_side[target]
        for inner_k in range(target):
            running = running - factor[target, inner_k] * interim[inner_k]
        interim.append(running / factor[target, target])
    solved = [None] * param_count
    for target in reversed(range(param_count)):
        running = interim[target]
        for inner_k in range(target + 1, param_count):
            running = running - factor[inner_k, target] * solved[inner_k]
        solved[target] = running / factor[target, target]
    return jnp.stack(solved)


def plain_body(spectra, inverse_var, mask_bits, sky_flags, fiber_ids, positions, throughput):
    exposures, fiber_count, wave_count = spectra.shape
    row_count = exposures * fiber_count
    coord_x = positions[0][fiber_ids]
    coord_y = positions[1][fiber_ids]

    def stack(first, second, scale):
        basis = jnp.stack([x * y for x in first for y in second], axis=-1)
        return (scale[:, :, None] * basis[None]).reshape(row_count, -1)

    design = stack(legendre(coord_x), legendre(coord_y), throughput)
    products = stack(
        legendre_series(coord_x, moment_degrees),
        legendre_series(coord_y, moment_degrees),
        throughput * throughput,
    )
    flux_rows = spectra.reshape(row_count, wave_count)
    usable = (mask_bits.reshape(row_count, wave_count) & bad_bits == 0).astype(jnp.float32)
    noise_weight = inverse_var.reshape(row_count, wave_count) * usable
    fit_weights = noise_weight * sky_flags.reshape(row_count).astype(jnp.float32)[:, None]
    normal = jnp.dot(products.T, fit_weights, precision=highest)
    right_side = jnp.dot(design.T, fit_weights * flux_rows, precision=highest)
    normal, right_side = lax.psum((normal, right_side), "fiber")
    normal = jnp.dot(rebuild_table(moment_degrees), normal, precision=highest)
    sky_coeffs = solve_normal(normal, right_side)
    residual = flux_rows - jnp.dot(design, sky_coeffs, precision=highest)
    chi_local = jnp.sum(noise_weight * residual * residual, axis=1)
    chi_total = lax.psum(chi_local, "wave")
    chi_square = (chi_total / (wave_count * lax.axis_size("wave"))).reshape(exposures, fiber_count)
    return (residual.reshape(exposures, fiber_count, wave_count), chi_square, sky_coeffs)


def choose_body(fiber_size, wave_size, spectra, *rest):
    exposures, fibers, waves = spectra.shape
    whole = fiber_size % low_size == 0 and fiber_size > low_size and wave_size == 2
    if whole and fibers % 8 == 0 and fibers <= lanes and exposures <= 8:
        for slices in (2, 1):
            if waves % (slices * fiber_size * lanes) == 0:
                return fused_body(fiber_size, wave_size, slices, spectra, *rest)
    return plain_body(spectra, *rest)


def solution(mesh):
    placed = (
        P(None, "fiber", "wave"),
        P(None, "fiber", "wave"),
        P(None, "fiber", "wave"),
        P(None, "fiber"),
        P("fiber"),
        P(),
        P(None, "fiber"),
    )
    return jax.shard_map(
        functools.partial(choose_body, mesh.shape["fiber"], mesh.shape["wave"]),
        mesh=mesh,
        in_specs=placed,
        out_specs=(P(None, "fiber", "wave"), P(None, "fiber"), P(None, "wave")),
        check_vma=False,
    )
```

time: 188 us -> 48.6 us (0.26)
  waiting for transfers between devices: 116 us -> 0 us
  Pallas kernels: 0 us -> 36 us
  other arithmetic: 34.3 us -> 0 us
  matrix products: 15.7 us -> 0 us
  between operations: 14.2 us -> 0.66 us
  local copies, waits for them, and re-layouts: 4.25 us -> 11.6 us
  blocking collectives: 2.44 us -> 0 us
    psum x1 -> x0, waiting for transfers between devices: 116 us -> none  [body(): normal, right_side = lax.psum((normal, right_side), 'fiber')]
    pallas_call x0 -> x1, Pallas kernels: none -> 36 us  [fused_body(): pl.pallas_call(functools.partial(kernel, fiber_size, wave_size, slices),...]
    div x11 -> x0, other arithmetic: 26.6 us -> none  [the longest x6 11.8 us: solve_normal(): solved[target] = running / factor[target, target]]
    dot_general x4 -> x0, matrix products: 15.7 us -> none  [the longest x1 5.83 us: body(): residual = flux_rows - jnp.dot(design, sky_coeffs, precision=highest)]
    unnamed x10 -> x19, local copies, waits for them, and re-layouts: 0.29 us -> 11.6 us
    mul x4 -> x0, other arithmetic: 4.51 us -> none  [the longest x1 3.03 us: body(): noise_weight = inverse_var.reshape(row_count, wave_count) * usable]
    psum x1 -> x0, blocking collectives: 2.44 us -> none  [body(): chi_total = lax.psum(chi_local, 'wave')]
  transfers between devices with their start and end apart: 1 -> 0, of which waited for: 1 -> 0; matrix products, arithmetic and copies ran while one was open for 0% -> 0% of each run, Pallas kernels for 0% -> 0%
where the time goes in v1:
time: 48.6 us; the launch traced here: 48.3 us
  Pallas kernels  36 us (74%)
  local copies, waits for them, and re-layouts  11.6 us (24%)
  between operations  0.66 us (1%)
    pallas_call x1, Pallas kernels, fused_body(): pl.pallas_call(functools.partial(kernel, fiber_size, wave_size, slices),...  36 us
    unnamed x19, local copies, waits for them, and re-layouts  11.6 us

profile of v1, /device:TPU:0, one launch (start us, length us, event | category | flops | bytes accessed | tf_op | source)
XLA Modules:
  0.0 48.3 jit_solution(8836022916037517063)
XLA Ops:
  0.6 0.0 copy-start
  0.6 1.7 %copy-done = f32[4,40,4096]{2,1,0:T(8,128)S(1)} copy-done((f32[4,40,4096]{2,1,0:T(8,128)S(1)}, f32[4,40,4096]{2,1,0:T(8,128)}, u32[]{:S(2)}) %copy-start) | copy-done | bytes 2621464
  2.4 0.0 copy-start.1
  2.4 1.7 %copy-done.1 = f32[4,40,4096]{2,1,0:T(8,128)S(1)} copy-done((f32[4,40,4096]{2,1,0:T(8,128)S(1)}, f32[4,40,4096]{2,1,0:T(8,128)}, u32[]{:S(2)}) %copy-start.1) | copy-done | bytes 2621464
  4.1 0.0 copy-start.2
  4.1 1.7 %copy-done.2 = s32[4,40,4096]{2,1,0:T(8,128)S(1)} copy-done((s32[4,40,4096]{2,1,0:T(8,128)S(1)}, s32[4,40,4096]{2,1,0:T(8,128)}, u32[]{:S(2)}) %copy-start.2) | copy-done | bytes 2621464
  5.9 0.0 copy-start.3
  5.9 0.9 %copy-done.3 = f32[256,56]{1,0:T(8,128)S(1)} copy-done((f32[256,56]{1,0:T(8,128)S(1)}, f32[256,56]{1,0:T(8,128)}, u32[]{:S(2)}) %copy-start.3) | copy-done | bytes 57368
  6.8 0.0 copy-start.4
  6.8 0.7 %copy-done.4 = f32[2,640]{1,0:T(2,128)S(1)} copy-done((f32[2,640]{1,0:T(2,128)S(1)}, f32[2,640]{1,0:T(2,128)}, u32[]{:S(2)}) %copy-start.4) | copy-done | bytes 5144
  7.4 0.0 copy-start.5
  7.5 0.7 %copy-done.5 = f32[4,40]{1,0:T(4,128)S(1)} copy-done((f32[4,40]{1,0:T(4,128)S(1)}, f32[4,40]{1,0:T(4,128)}, u32[]{:S(2)}) %copy-start.5) | copy-done | bytes 664
  8.1 0.0 copy-start.6
  8.1 0.7 %copy-done.6 = s32[4,40]{1,0:T(4,128)S(1)} copy-done((s32[4,40]{1,0:T(4,128)S(1)}, s32[4,40]{1,0:T(4,128)}, u32[]{:S(2)}) %copy-start.6) | copy-done | bytes 664
  8.8 0.0 copy-start.7
  8.8 0.7 %copy-done.7 = s32[40]{0:T(128)S(1)} copy-done((s32[40]{0:T(128)S(1)}, s32[40]{0:T(128)}, u32[]{:S(2)}) %copy-start.7) | copy-done | bytes 184
  9.5 36.0 %shard_map.103 = (f32[4,40,4096]{2,1,0:T(8,128)S(1)}, f32[4,40]{1,0:T(4,128)S(1)}, f32[16,4096]{1,0:T(8,128)S(1)}) custom-call(s32[1,40]{1,0:T(1,128)S(1)} %bitcast.1, f32[2,640]{1,0:T(2,128)S(1)} %copy-done.4, f32[4,40]{1,0:T(4,128)S(1)} %copy-done.5, s32[4,40]{1,0:T(4,128)S(1)} %copy-done.6, f32[256,56]{1,0:T(8,128)S(1)} %copy-done.3, ...), custom_call_target="tpu_custom_call" | custom-call | tf_op jit(solution)/shard_map/pallas_call | solution.py:379
  45.5 1.5 %copy.14 = f32[4,40,4096]{2,1,0:T(8,128)} copy(f32[4,40,4096]{2,1,0:T(8,128)S(1)} %get-tuple-element.6) | data formatting | bytes 5242880
  47.0 0.6 %copy.15 = f32[4,40]{1,0:T(4,128)} copy(f32[4,40]{1,0:T(4,128)S(1)} %get-tuple-element.7) | data formatting | bytes 1280
  47.6 0.7 %copy.16 = f32[16,4096]{1,0:T(8,128)} copy(f32[16,4096]{1,0:T(8,128)S(1)} %get-tuple-element.8) | data formatting | bytes 524288
Async XLA Ops:
  0.6 1.7 %copy-start = (f32[4,40,4096]{2,1,0:T(8,128)S(1)}, f32[4,40,4096]{2,1,0:T(8,128)}, u32[]{:S(2)}) copy-start(f32[4,40,4096]{2,1,0:T(8,128)} %spectra_hbm.1) | copy-start | bytes 7864324
  2.4 1.7 %copy-start.1 = (f32[4,40,4096]{2,1,0:T(8,128)S(1)}, f32[4,40,4096]{2,1,0:T(8,128)}, u32[]{:S(2)}) copy-start(f32[4,40,4096]{2,1,0:T(8,128)} %ivar_hbm.1) | copy-start | bytes 7864324
  4.1 1.7 %copy-start.2 = (s32[4,40,4096]{2,1,0:T(8,128)S(1)}, s32[4,40,4096]{2,1,0:T(8,128)}, u32[]{:S(2)}) copy-start(s32[4,40,4096]{2,1,0:T(8,128)} %bits_hbm.1) | copy-start | bytes 7864324
  5.9 0.9 %copy-start.3 = (f32[256,56]{1,0:T(8,128)S(1)}, f32[256,56]{1,0:T(8,128)}, u32[]{:S(2)}) copy-start(f32[256,56]{1,0:T(8,128)} %constant.2.clone.table_ref) | copy-start | bytes 172036
  6.8 0.7 %copy-start.4 = (f32[2,640]{1,0:T(2,128)S(1)}, f32[2,640]{1,0:T(2,128)}, u32[]{:S(2)}) copy-start(f32[2,640]{1,0:T(2,128)} %positions_ref.1) | copy-start | bytes 15364
  7.4 0.7 %copy-start.5 = (f32[4,40]{1,0:T(4,128)S(1)}, f32[4,40]{1,0:T(4,128)}, u32[]{:S(2)}) copy-start(f32[4,40]{1,0:T(4,128)} %throughput_ref.1) | copy-start | bytes 1924
  8.1 0.7 %copy-start.6 = (s32[4,40]{1,0:T(4,128)S(1)}, s32[4,40]{1,0:T(4,128)}, u32[]{:S(2)}) copy-start(s32[4,40]{1,0:T(4,128)} %flags_ref.1) | copy-start | bytes 1924
  8.8 0.7 %copy-start.7 = (s32[40]{0:T(128)S(1)}, s32[40]{0:T(128)}, u32[]{:S(2)}) copy-start(s32[40]{0:T(128)} %param.12) | copy-start | bytes 484

commit v2 on v1

--- a/solution.py
+++ b/solution.py
@@ -16,7 +16,6 @@
 basis_degrees = 4
 padded_degrees = 8
 moment_rows = moment_degrees * padded_degrees
-all_rows = moment_rows + PARAMS
 lanes = 128
 low_size = 4
 MESH = pl.DeviceIdType.MESH
@@ -150,10 +149,9 @@
     return moments, design * flags, design
 
 
-def solve_block(table, summed):
-    width = summed.shape[1]
-    normal = exact_dot(table, summed[:moment_rows])
-    right = summed[moment_rows:]
+def solve_block(table, moments, right):
+    width = right.shape[1]
+    normal = exact_dot(table, moments)
     sub = iota((PARAMS, width), 0)
     cols = [
         normal[k * PARAMS:(k + 1) * PARAMS] + jnp.where(sub == k, prior_weight, 0.0)
@@ -181,12 +179,14 @@
 
 def kernel(
     fiber_size, wave_size, slices,
+    ids_hbm, positions_hbm, throughput_hbm, flags_hbm, table_hbm,
+    spectra_hbm, ivar_hbm, bits_hbm,
+    residual_ref, chi_ref, coeffs_ref,
     ids_ref, positions_ref, throughput_ref, flags_ref, table_ref,
-    spectra_hbm, ivar_hbm, bits_hbm,
-    residual_hbm, chi_ref, coeffs_ref,
-    flux, noise, bits, resid, moments, gather1, partial, gather2, coeffs,
+    flux, noise, bits, moments, gather1, partial, gather2,
+    rights, right_gather1, right_partial, right_gather2, coeffs,
     chi_mine, chi_other,
-    load_sem, store_sem, send_sem, recv_sem, chi_sem,
+    small_sem, load_sem, send_sem, recv_sem, chi_sem,
 ):
     exposures, fibers, waves = flux.shape
     rows = exposures * fibers
@@ -210,6 +210,14 @@
         group = lax.rem(low + d, low_size)
         return group, pl.ds(pl.multiple_of(s * low_size * chunk + group * chunk, chunk), chunk)
 
+    small = []
+    for n, (source, target) in enumerate((
+        (ids_hbm, ids_ref), (positions_hbm, positions_ref), (throughput_hbm, throughput_ref),
+        (flags_hbm, flags_ref), (table_hbm, table_ref),
+    )):
+        copy = pltpu.make_async_copy(source, target, small_sem.at[n])
+        copy.start()
+        small.append(copy)
     loads = []
     for at, (s, d) in enumerate(order):
         where = span(s, d)[1]
@@ -224,6 +232,8 @@
             copies.append(copy)
         loads.append(copies)
 
+    for copy in small:
+        copy.wait()
     feature, right_feature, design = build_features(
         ids_ref, positions_ref, throughput_ref, flags_ref
     )
@@ -241,7 +251,7 @@
         )
 
     started = []
-    first = {}
+    first, right_first = {}, {}
     for at, (s, d) in enumerate(order):
         group, where = span(s, d)
         for copy in loads[at]:
@@ -254,18 +264,41 @@
         right = exact_dot(right_feature, scaled)
         for b in range(high_size):
             lane = slice(b * block, (b + 1) * block)
-            moments[s, group, b, :moment_rows] = normal[:, lane]
-            moments[s, group, b, moment_rows:] = right[:, lane]
+            moments[s, group, b] = normal[:, lane]
+            rights[s, b, group] = right[:, lane]
         if d:
             copy = remote(0, s, d, moments.at[s, group], gather1.at[s, d - 1], low_peer[d])
             copy.start()
             started.append(copy)
             first[s, d] = copy
-
-    def reduce_low(s):
+        else:
+            for e in range(1, high_size):
+                to = lax.rem(high + e, high_size)
+                copy = remote(
+                    4, s, e, rights.at[s, to], right_gather1.at[s, e - 1], high_peer[e]
+                )
+                copy.start()
+                started.append(copy)
+                right_first[s, e] = copy
+
+    def reduce_first(s):
+        copies = []
+        for e in range(1, high_size):
+            right_first[s, e].wait_recv()
+        for d in list(range(1, low_size)) + [0]:
+            to = lax.rem(low + d, low_size)
+            total = rights[s, high, to]
+            for e in range(high_size - 1):
+                total = total + right_gather1[s, e, to]
+            right_partial[s, to] = total
+            if d:
+                copy = remote(
+                    5, s, d, right_partial.at[s, to], right_gather2.at[s, d - 1], low_peer[d]
+                )
+                copy.start()
+                copies.append(copy)
         for d in range(1, low_size):
             first[s, d].wait_recv()
-        copies = []
         for d in list(range(1, high_size)) + [0]:
             to = lax.rem(high + d, high_size)
             total = moments[s, low, to]
@@ -279,13 +312,16 @@
         started.extend(copies)
         return copies
 
-    def reduce_high(s, copies):
+    def reduce_second(s, copies):
         for copy in copies:
             copy.wait_recv()
         total = partial[s, high]
         for e in range(high_size - 1):
             total = total + gather2[s, e]
-        solved = solve_block(table_ref[...], total)
+        right = right_partial[s, low]
+        for e in range(low_size - 1):
+            right = right + right_gather2[s, e]
+        solved = solve_block(table_ref[...], total, right)
         mine = coeffs.at[s, low * high_size + high]
         mine[...] = solved
         copies = []
@@ -308,7 +344,6 @@
         started.extend(copies)
         return copies
 
-    stores = []
     chi_total = [jnp.zeros((rows, lanes), jnp.float32)]
 
     def finish(s, copies):
@@ -328,23 +363,17 @@
                 preferred_element_type=jnp.float32,
             )
             left = flux[:, :, where].reshape(rows, chunk) - model
-            resid[:, :, where] = left.reshape(exposures, fibers, chunk)
+            residual_ref[:, :, where] = left.reshape(exposures, fibers, chunk)
             term = noise[:, :, where].reshape(rows, chunk) * left * left
             for n in range(chunk // lanes):
                 chi_total[0] = chi_total[0] + term[:, n * lanes:(n + 1) * lanes]
-            copy = pltpu.make_async_copy(
-                resid.at[:, :, where], residual_hbm.at[:, :, where],
-                store_sem.at[s * low_size + group],
-            )
-            copy.start()
-            stores.append(copy)
 
     stage = {}
-    stage[0] = reduce_high(0, reduce_low(0))
+    stage[0] = reduce_second(0, reduce_first(0))
     for s in range(1, slices):
-        following = reduce_low(s)
+        following = reduce_first(s)
         stage[s - 1] = spread_low(s - 1, stage[s - 1])
-        stage[s] = reduce_high(s, following)
+        stage[s] = reduce_second(s, following)
         finish(s - 1, stage[s - 1])
     finish(slices - 1, spread_low(slices - 1, stage[slices - 1]))
 
@@ -361,8 +390,6 @@
     copy.wait()
     both = chi_mine[:exposures, :fibers] + chi_other[:exposures, :fibers]
     chi_ref[...] = both / (waves * wave_size)
-    for copy in stores:
-        copy.wait()
     for copy in started:
         copy.wait_send()
 
@@ -374,7 +401,6 @@
     block = waves // (slices * fiber_size)
     table = rebuild_table(padded_degrees)
     vmem = pl.BlockSpec(memory_space=pltpu.VMEM)
-    anywhere = pl.BlockSpec(memory_space=pl.ANY)
     cube = (exposures, fibers, waves)
     residual, chi, coeffs = pl.pallas_call(
         functools.partial(kernel, fiber_size, wave_size, slices),
@@ -383,31 +409,42 @@
             jax.ShapeDtypeStruct((exposures, fibers), jnp.float32),
             jax.ShapeDtypeStruct((PARAMS, waves), jnp.float32),
         ),
-        in_specs=[vmem] * 5 + [anywhere] * 3,
-        out_specs=(anywhere, vmem, vmem),
+        in_specs=[pl.BlockSpec(memory_space=pltpu.HBM)] * 8,
+        out_specs=(vmem, vmem, vmem),
         scratch_shapes=[
+            pltpu.VMEM((1, fibers), jnp.int32),
+            pltpu.VMEM(positions.shape, jnp.float32),
+            pltpu.VMEM((exposures, fibers), jnp.float32),
+            pltpu.VMEM((exposures, fibers), jnp.int32),
+            pltpu.VMEM(table.shape, jnp.float32),
             pltpu.VMEM(cube, jnp.float32),
             pltpu.VMEM(cube, jnp.float32),
             pltpu.VMEM(cube, jnp.int32),
-            pltpu.VMEM(cube, jnp.float32),
-            pltpu.VMEM((slices, low_size, high_size, all_rows, block), jnp.float32),
-            pltpu.VMEM((slices, low_size - 1, high_size, all_rows, block), jnp.float32),
-            pltpu.VMEM((slices, high_size, all_rows, block), jnp.float32),
-            pltpu.VMEM((slices, high_size - 1, all_rows, block), jnp.float32),
+            pltpu.VMEM((slices, low_size, high_size, moment_rows, block), jnp.float32),
+            pltpu.VMEM((slices, low_size - 1, high_size, moment_rows, block), jnp.float32),
+            pltpu.VMEM((slices, high_size, moment_rows, block), jnp.float32),
+            pltpu.VMEM((slices, high_size - 1, moment_rows, block), jnp.float32),
+            pltpu.VMEM((slices, high_size, low_size, PARAMS, block), jnp.float32),
+            pltpu.VMEM((slices, high_size - 1, low_size, PARAMS, block), jnp.float32),
+            pltpu.VMEM((slices, low_size, PARAMS, block), jnp.float32),
+            pltpu.VMEM((slices, low_size - 1, PARAMS, block), jnp.float32),
             pltpu.VMEM((slices, fiber_size, PARAMS, block), jnp.float32),
             pltpu.VMEM((8, lanes), jnp.float32),
             pltpu.VMEM((8, lanes), jnp.float32),
+            pltpu.SemaphoreType.DMA((5,)),
             pltpu.SemaphoreType.DMA((slices * low_size, 3)),
-            pltpu.SemaphoreType.DMA((slices * low_size,)),
-            pltpu.SemaphoreType.DMA((slices, 4, max(low_size, high_size) - 1)),
-            pltpu.SemaphoreType.DMA((slices, 4, max(low_size, high_size) - 1)),
+            pltpu.SemaphoreType.DMA((slices, 6, max(low_size, high_size) - 1)),
+            pltpu.SemaphoreType.DMA((slices, 6, max(low_size, high_size) - 1)),
             pltpu.SemaphoreType.DMA((2,)),
         ],
         compiler_params=pltpu.CompilerParams(
             collective_id=0, has_side_effects=True, vmem_limit_bytes=40 * 1024 * 1024
         ),
-    )(fiber_ids.reshape(1, fibers), positions, throughput, sky_flags, table,
-      spectra, inverse_var, mask_bits)
+    )(*[
+        pltpu.with_memory_space_constraint(value, pltpu.HBM)
+        for value in (fiber_ids.reshape(1, fibers), positions, throughput, sky_flags, table,
+                      spectra, inverse_var, mask_bits)
+    ])
     return residual, chi, coeffs
 
 

time: 48.6 us -> 39.6 us (0.81)
  local copies, waits for them, and re-layouts: 11.6 us -> 2.77 us
    unnamed x19 -> x3, local copies, waits for them, and re-layouts: 11.6 us -> 2.77 us
where the time goes in v2:
time: 39.6 us; the launch traced here: 39.5 us
  Pallas kernels  36 us (91%)
  local copies, waits for them, and re-layouts  2.77 us (7%)
  between operations  0.64 us (2%)
    pallas_call x1, Pallas kernels, fused_body(): pl.pallas_call(functools.partial(kernel, fiber_size, wave_size, slices),...  36 us
    unnamed x3, local copies, waits for them, and re-layouts  2.77 us

profile of v2, /device:TPU:0, one launch (start us, length us, event | category | flops | bytes accessed | tf_op | source)
XLA Modules:
  0.0 39.5 jit_solution(10400602417399456395)
XLA Ops:
  0.6 36.0 %shard_map.103 = (f32[4,40,4096]{2,1,0:T(8,128)S(1)}, f32[4,40]{1,0:T(4,128)S(1)}, f32[16,4096]{1,0:T(8,128)S(1)}) custom-call(s32[1,40]{1,0:T(1,128)} %bitcast.1, f32[2,640]{1,0:T(2,128)} %positions_hbm.1, f32[4,40]{1,0:T(4,128)} %throughput_hbm.1, s32[4,40]{1,0:T(4,128)} %flags_hbm.1, f32[256,56]{1,0:T(8,128)} %constant.2.clone.table_hbm, ...), custom_call_target="tpu_custom_call" | custom-call | tf_op jit(solution)/shard_map/pallas_call | solution.py:405
  36.7 1.5 %copy.14 = f32[4,40,4096]{2,1,0:T(8,128)} copy(f32[4,40,4096]{2,1,0:T(8,128)S(1)} %get-tuple-element.6) | data formatting | bytes 5242880
  38.2 0.6 %copy.15 = f32[4,40]{1,0:T(4,128)} copy(f32[4,40]{1,0:T(4,128)S(1)} %get-tuple-element.7) | data formatting | bytes 1280
  38.8 0.7 %copy.16 = f32[16,4096]{1,0:T(8,128)} copy(f32[16,4096]{1,0:T(8,128)S(1)} %get-tuple-element.8) | data formatting | bytes 524288

commit v3 on v2

--- a/solution.py
+++ b/solution.py
@@ -14,8 +14,9 @@
 highest = lax.Precision.HIGHEST
 moment_degrees = 7
 basis_degrees = 4
-padded_degrees = 8
-moment_rows = moment_degrees * padded_degrees
+moment_rows = moment_degrees * moment_degrees
+lead_rows = moment_rows // 8 * 8
+sent_rows = lead_rows + 8
 lanes = 128
 low_size = 4
 MESH = pl.DeviceIdType.MESH
@@ -134,12 +135,19 @@
     flags = widen(flags_ref[...].astype(jnp.float32))
     series_x = legendre_series(coord_x, moment_degrees)
     series_y = legendre_series(coord_y, moment_degrees)
-    sub = iota((padded_degrees, rows), 0)
-    stack_y = jnp.zeros((padded_degrees, rows), jnp.float32)
+    scale = through * through * flags
+    sub = iota((moment_rows, rows), 0)
+    moments = jnp.zeros((moment_rows, rows), jnp.float32)
+    spread_y = jnp.zeros((moment_rows, rows), jnp.float32)
     for order in range(moment_degrees):
-        stack_y = jnp.where(sub == order, series_y[order], stack_y)
-    scale = through * through * flags
-    moments = jnp.concatenate([stack_y * (one * scale) for one in series_x], axis=0)
+        first_row = order * moment_degrees
+        in_x = (sub >= first_row) & (sub < first_row + moment_degrees)
+        moments = jnp.where(in_x, series_x[order] * scale, moments)
+        in_y = functools.reduce(
+            jnp.logical_or, [sub == a * moment_degrees + order for a in range(moment_degrees)]
+        )
+        spread_y = jnp.where(in_y, series_y[order], spread_y)
+    moments = moments * spread_y
     poly_x, poly_y = legendre(coord_x), legendre(coord_y)
     sub = iota((PARAMS, rows), 0)
     design = jnp.zeros((PARAMS, rows), jnp.float32)
@@ -151,7 +159,7 @@
 
 def solve_block(table, moments, right):
     width = right.shape[1]
-    normal = exact_dot(table, moments)
+    normal = exact_dot(table, moments[:moment_rows])
     sub = iota((PARAMS, width), 0)
     cols = [
         normal[k * PARAMS:(k + 1) * PARAMS] + jnp.where(sub == k, prior_weight, 0.0)
@@ -250,6 +258,7 @@
             device_id={"fiber": peer}, device_id_type=MESH,
         )
 
+    tail_row = high_size * lead_rows
     started = []
     first, right_first = {}, {}
     for at, (s, d) in enumerate(order):
@@ -264,7 +273,8 @@
         right = exact_dot(right_feature, scaled)
         for b in range(high_size):
             lane = slice(b * block, (b + 1) * block)
-            moments[s, group, b] = normal[:, lane]
+            moments[s, group, b * lead_rows:(b + 1) * lead_rows] = normal[:lead_rows, lane]
+            moments[s, group, tail_row + b:tail_row + b + 1] = normal[lead_rows:moment_rows, lane]
             rights[s, b, group] = right[:, lane]
         if d:
             copy = remote(0, s, d, moments.at[s, group], gather1.at[s, d - 1], low_peer[d])
@@ -301,10 +311,14 @@
             first[s, d].wait_recv()
         for d in list(range(1, high_size)) + [0]:
             to = lax.rem(high + d, high_size)
-            total = moments[s, low, to]
+            lead = pl.ds(pl.multiple_of(to * lead_rows, 8), lead_rows)
+            tail = pl.ds(tail_row + to, 1)
+            total, last = moments[s, low, lead], moments[s, low, tail]
             for e in range(low_size - 1):
-                total = total + gather1[s, e, to]
-            partial[s, to] = total
+                total = total + gather1[s, e, lead]
+                last = last + gather1[s, e, tail]
+            partial[s, to, :lead_rows] = total
+            partial[s, to, lead_rows:] = jnp.broadcast_to(last, (8, block))
             if d:
                 copy = remote(1, s, d, partial.at[s, to], gather2.at[s, d - 1], high_peer[d])
                 copy.start()
@@ -347,11 +361,10 @@
     chi_total = [jnp.zeros((rows, lanes), jnp.float32)]
 
     def finish(s, copies):
-        for copy in copies:
-            copy.wait_recv()
-        for group in range(low_size):
-            start = (s * low_size + group) * chunk
-            where = pl.ds(start, chunk)
+        for d in range(low_size):
+            if d:
+                copies[d - 1].wait_recv()
+            group, where = span(s, low_size - d)
             values = jnp.concatenate(
                 [coeffs[s, group * high_size + b] for b in range(high_size)], axis=1
             )
@@ -399,7 +412,8 @@
     exposures, fibers, waves = spectra.shape
     high_size = fiber_size // low_size
     block = waves // (slices * fiber_size)
-    table = rebuild_table(padded_degrees)
+    table = rebuild_table(moment_degrees)
+    group_rows = high_size * lead_rows + -(-high_size // 8) * 8
     vmem = pl.BlockSpec(memory_space=pltpu.VMEM)
     cube = (exposures, fibers, waves)
     residual, chi, coeffs = pl.pallas_call(
@@ -420,10 +434,10 @@
             pltpu.VMEM(cube, jnp.float32),
             pltpu.VMEM(cube, jnp.float32),
             pltpu.VMEM(cube, jnp.int32),
-            pltpu.VMEM((slices, low_size, high_size, moment_rows, block), jnp.float32),
-            pltpu.VMEM((slices, low_size - 1, high_size, moment_rows, block), jnp.float32),
-            pltpu.VMEM((slices, high_size, moment_rows, block), jnp.float32),
-            pltpu.VMEM((slices, high_size - 1, moment_rows, block), jnp.float32),
+            pltpu.VMEM((slices, low_size, group_rows, block), jnp.float32),
+            pltpu.VMEM((slices, low_size - 1, group_rows, block), jnp.float32),
+            pltpu.VMEM((slices, high_size, sent_rows, block), jnp.float32),
+            pltpu.VMEM((slices, high_size - 1, sent_rows, block), jnp.float32),
             pltpu.VMEM((slices, high_size, low_size, PARAMS, block), jnp.float32),
             pltpu.VMEM((slices, high_size - 1, low_size, PARAMS, block), jnp.float32),
             pltpu.VMEM((slices, low_size, PARAMS, block), jnp.float32),

time: 39.6 us -> 39.2 us (0.990)
  Pallas kernels: 36 us -> 35.6 us
    pallas_call x1, Pallas kernels: 36 us -> 35.6 us  [fused_body(): pl.pallas_call(functools.partial(kernel, fiber_size, wave_size, slices),...]
where the time goes in v3:
time: 39.2 us; the launch traced here: 39 us
  Pallas kernels  35.6 us (91%)
  local copies, waits for them, and re-layouts  2.77 us (7%)
  between operations  0.64 us (2%)
    pallas_call x1, Pallas kernels, fused_body(): pl.pallas_call(functools.partial(kernel, fiber_size, wave_size, slices),...  35.6 us
    unnamed x3, local copies, waits for them, and re-layouts  2.77 us

profile of v3, /device:TPU:0, one launch (start us, length us, event | category | flops | bytes accessed | tf_op | source)
XLA Modules:
  0.0 39.0 jit_solution(15816361289402854168)
XLA Ops:
  0.6 35.6 %shard_map.103 = (f32[4,40,4096]{2,1,0:T(8,128)S(1)}, f32[4,40]{1,0:T(4,128)S(1)}, f32[16,4096]{1,0:T(8,128)S(1)}) custom-call(s32[1,40]{1,0:T(1,128)} %bitcast.1, f32[2,640]{1,0:T(2,128)} %positions_hbm.1, f32[4,40]{1,0:T(4,128)} %throughput_hbm.1, s32[4,40]{1,0:T(4,128)} %flags_hbm.1, f32[256,49]{1,0:T(8,128)} %constant.2.clone.table_hbm, ...), custom_call_target="tpu_custom_call" | custom-call | tf_op jit(solution)/shard_map/pallas_call | solution.py:419
  36.3 1.5 %copy.14 = f32[4,40,4096]{2,1,0:T(8,128)} copy(f32[4,40,4096]{2,1,0:T(8,128)S(1)} %get-tuple-element.6) | data formatting | bytes 5242880
  37.8 0.6 %copy.15 = f32[4,40]{1,0:T(4,128)} copy(f32[4,40]{1,0:T(4,128)S(1)} %get-tuple-element.7) | data formatting | bytes 1280
  38.3 0.7 %copy.16 = f32[16,4096]{1,0:T(8,128)} copy(f32[16,4096]{1,0:T(8,128)S(1)} %get-tuple-element.8) | data formatting | bytes 524288
